TPU v7x, 32 devices: a whole 2x2x4 slice. The times are simulated.
32 devices in a mesh: ctx: 8 (over y, x, core), ch: 4 (over z).
Axes of the slice: x: 2, y: 2, z: 4, core: 2. Of those that a mesh axis runs over, the one named last changes fastest.
Arguments:
- query_act: bfloat16 [4096, 4096], P('ctx', 'ch'), may hold values from -6 to 6
- key_act: bfloat16 [4096, 4096], P('ctx', 'ch'), may hold values from -6 to 6
- value_act: bfloat16 [4096, 4096], P('ctx', 'ch'), may hold values from -6 to 6
- filters: bfloat16 [4096, 128], P('ch'), may hold values from -0.5 to 0.5
- proj_weight: bfloat16 [8192, 4096], P('ctx', 'ch'), may hold values from -0.09375 to 0.09375
- cotangent: bfloat16 [4096, 8192], P('ctx', 'ch'), may hold values from -6 to 6
Outputs:
- grad_query: bfloat16 [4096, 4096], P('ctx', 'ch')
- grad_key: bfloat16 [4096, 4096], P('ctx', 'ch')
- grad_value: bfloat16 [4096, 4096], P('ctx', 'ch')
- grad_filter: float32 [4096, 128], P('ch')
- grad_proj: float32 [8192, 4096], P('ctx', 'ch')
All inputs are finite; a program needn't handle non-finite values.
Results may differ from a plain program's by a relative error of at most 0.0051.
Values may be sent and summed in bfloat16 or wider, within the bound.
A program may use at most 192 MiB of HBM per device.

v0:
```python
import jax
import jax.numpy as jnp
from jax import lax
from jax.sharding import PartitionSpec as P

TAPS = 128


def from_behind(x, axis, by):
    length = lax.axis_size(axis)
    pairs = [(i, i + by) for i in range(length) if 0 <= i + by < length]
    return lax.ppermute(x, axis, pairs)


def tap_sum(filt_f, extended, tokens, causal):
    group_width = 8
    group_count = TAPS // group_width
    channels = extended.shape[1]

    def tap_one_group(group_index, total):
        group_start = group_index.astype(jnp.int32) * group_width
        if causal:
            first = jnp.int32(TAPS - group_width) - group_start
        else:
            first = group_start
        slab = lax.dynamic_slice_in_dim(extended, first, tokens + group_width - 1, 0).astype(
            jnp.float32
        )
        weights = lax.dynamic_slice_in_dim(filt_f, group_start, group_width, 1)
        for inner in range(group_width):
            if causal:
                begin = group_width - 1 - inner
            else:
                begin = inner
            total = total + weights[:, inner][None, :] * slab[begin : begin + tokens]
        return total

    return lax.fori_loop(0, group_count, tap_one_group, jnp.zeros((tokens, channels), jnp.float32))


def filter_sums(grad_gate, lagged):
    tokens = grad_gate.shape[0]
    group_width = 8
    group_count = TAPS // group_width
    gate_f = grad_gate.astype(jnp.float32)

    def filter_one_group(group_index):
        first = jnp.int32(TAPS - group_width) - group_index * group_width
        lag_slab = lax.dynamic_slice_in_dim(lagged, first, tokens + group_width - 1, 0).astype(
            jnp.float32
        )
        stacked = jnp.stack(
            [
                lag_slab[group_width - 1 - inner : group_width - 1 - inner + tokens]
                for inner in range(group_width)
            ],
            0,
        )
        return jnp.sum(stacked * gate_f[None], axis=1)

    sums = lax.map(filter_one_group, jnp.arange(group_count, dtype=jnp.int32))
    return sums.reshape(TAPS, grad_gate.shape[1]).T


def shards(query_act, key_act, value_act, filters, proj_weight, cotangent):
    tokens = query_act.shape[0]
    gathered = lax.all_gather(cotangent, "ch", axis=1, tiled=True)
    query_f = query_act.astype(jnp.float32)
    key_f = key_act.astype(jnp.float32)
    value_f = value_act.astype(jnp.float32)
    filt_f = filters.astype(jnp.float32)
    product = (key_f * value_f).astype(jnp.bfloat16)
    before = from_behind(product[tokens - TAPS + 1 :], "ctx", 1)
    lagged = jnp.concatenate([before, product], 0)
    mixed = tap_sum(filt_f, lagged, tokens, True)
    gated = (query_f * mixed).astype(jnp.bfloat16)
    grad_mix = jnp.dot(
        gathered,
        lax.all_gather(proj_weight, "ctx", axis=0, tiled=True),
        preferred_element_type=jnp.float32,
    )
    grad_query = (grad_mix * mixed).astype(jnp.bfloat16)
    grad_gate = (grad_mix * query_f).astype(jnp.bfloat16)
    after = from_behind(grad_gate[: TAPS - 1], "ctx", -1)
    leading = jnp.concatenate([grad_gate, after], 0)
    grad_prod = tap_sum(filt_f, leading, tokens, False)
    grad_key = (grad_prod * value_f).astype(jnp.bfloat16)
    grad_value = (grad_prod * key_f).astype(jnp.bfloat16)
    local_filter = filter_sums(grad_gate, lagged)
    grad_filter = lax.psum(local_filter, "ctx")
    own_rows = proj_weight.shape[0]
    partial_grad = lax.dot_general(
        gathered, gated, (((0,), (0,)), ((), ())), preferred_element_type=jnp.float32
    )
    summed = lax.psum(partial_grad, "ctx")
    grad_proj = lax.dynamic_slice_in_dim(summed, lax.axis_index("ctx") * own_rows, own_rows, 0)
    return (grad_query, grad_key, grad_value, grad_filter, grad_proj)


def solution(mesh):
    return jax.shard_map(
        shards,
        mesh=mesh,
        in_specs=(
            P("ctx", "ch"),
            P("ctx", "ch"),
            P("ctx", "ch"),
            P("ch", None),
            P("ctx", "ch"),
            P("ctx", "ch"),
        ),
        out_specs=(P("ctx", "ch"), P("ctx", "ch"), P("ctx", "ch"), P("ch", None), P("ctx", "ch")),
        check_vma=False,
    )
```

profile of v0, /device:TPU:0, one launch (start us, length us, event | category | flops | bytes accessed | tf_op | source)
XLA Modules:
  0.0 1226.1 jit_solution(14841337921941511170)
XLA Ops:
  8.7 153.2 %all-gather.3.cloned.1.call-done = bf16[512,8192]{1,0:T(8,128)(2,1)} async-done(((bf16[512,2048]{1,0:T(8,128)(2,1)}), bf16[512,8192]{1,0:T(8,128)(2,1)}) %all-gather.3.cloned.1.call-update) | async-done | bytes 8388624 | tf_op jit(solution)/shard_map/all_gather | solution.py:67
  162.0 90.0 %all-gather.5.cloned.1.call-done = bf16[8192,1024]{1,0:T(8,128)(2,1)} async-done(((bf16[1024,1024]{1,0:T(8,128)(2,1)}), bf16[8192,1024]{1,0:T(8,128)(2,1)}) %all-gather.5.cloned.1.call-update) | async-done | bytes 16777232 | tf_op jit(solution)/shard_map/all_gather | solution.py:79
  251.9 16.1 %fusion.30 = (f32[512,1024]{1,0:T(8,128)}, bf16[512,1024]{1,0:T(8,128)(2,1)S(1)}, f32[512,1024]{1,0:T(8,128)}) fusion(bf16[512,1024]{1,0:T(8,128)(2,1)S(1)} %copy-done.2, bf16[512,8192]{1,0:T(8,128)(2,1)} %all-gather.3.cloned.1.call-done, bf16[8192,1024]{1,0:T(8,128)(2,1)} %all-gather.5.cloned.1.call-done), kind=kOutput, calls=%fused_computation.84 | convolution fusion | flops 8592031744 | bytes 31457280 | tf_op jit(solution)/shard_map/dot_general | solution.py:77
  271.6 90.8 %while.44 = (s32[]{:T(128)}, f32[512,1024]{1,0:T(8,128)}, f32[1024,128]{0,1:T(8,128)}, bf16[639,1024]{1,0:T(8,128)(2,1)S(1)}, s32[]{:T(128)}, /*index=5*/s32[]{:...) while((s32[]{:T(128)}, f32[512,1024]{1,0:T(8,128)}, ...), condition=%wide.region_3.0_spmd.clone, body=%wide.region_2.0_spmd.clone.sunk | while | flops 9444368 | bytes 24258916 | solution.py:38
  366.8 6.6 collective-permute-start
  374.6 91.0 %while.43 = (s32[]{:T(128)}, f32[512,1024]{1,0:T(8,128)}, f32[1024,128]{0,1:T(8,128)}, bf16[639,1024]{1,0:T(8,128)(2,1)S(1)}, s32[]{:T(128)}, /*index=5*/s32[]{:...) while((s32[]{:T(128)}, f32[512,1024]{1,0:T(8,128)}, ...), condition=%wide.region_1.0_spmd.clone, body=%wide.region_0.0_spmd.clone.sunk | while | flops 9444370 | bytes 24258944 | solution.py:38
  465.7 315.1 %while.42 = (s32[]{:T(128)}, f32[16,8,1024]{2,1,0:T(8,128)}, s32[16]{0:T(128)S(1)}, bf16[639,1024]{1,0:T(8,128)(2,1)S(1)}, f32[512,1024]{1,0:T(8,128)}, /*index=...) while((s32[]{:T(128)}, f32[16,8,1024]{2,1,0:T(8,128)}, s32[16]{0:T(128)S(1)}, ...), condition=%wide.region_6.7_spmd, body=%wide.region_4.6_spmd.sunk | while | flops 8911879 | bytes 122824920 | solution.py:61
  470.3 5.7 copy-done
  476.0 8.8 multiply_reduce_fusion.2
  489.9 5.7 copy-done
  495.7 8.8 multiply_reduce_fusion.2
  509.6 5.7 copy-done
  515.4 8.8 multiply_reduce_fusion.2
  529.3 5.7 copy-done
  535.0 8.8 multiply_reduce_fusion.2
  549.0 5.7 copy-done
  554.7 8.8 multiply_reduce_fusion.2
  568.7 5.7 copy-done
  574.4 8.8 multiply_reduce_fusion.2
  588.4 5.7 copy-done
  594.1 8.8 multiply_reduce_fusion.2
  613.8 8.8 multiply_reduce_fusion.2
  633.5 8.8 multiply_reduce_fusion.2
  653.2 8.8 multiply_reduce_fusion.2
  672.9 8.8 multiply_reduce_fusion.2
  692.6 8.8 multiply_reduce_fusion.2
  712.2 8.8 multiply_reduce_fusion.2
  731.9 8.8 multiply_reduce_fusion.2
  751.6 8.8 multiply_reduce_fusion.2
  771.3 8.8 multiply_reduce_fusion.2
  780.7 17.9 %convolution_bitcast_fusion = f32[8192,1024]{0,1:T(8,128)} fusion(bf16[512,8192]{1,0:T(8,128)(2,1)} %all-gather.3.cloned.1.call-done, f32[512,1024]{1,0:T(8,128)S(1)} %copy-done.1, bf16[512,1024]{1,0:T(8,128)(2,1)} %param.12), kind=kOutput, calls=%fused_computation.69 | convolution fusion | flops 8591507456 | bytes 45088768 | tf_op jit(solution)/shard_map/dot_general | solution.py:92
  801.5 405.9 %all-reduce.3.cloned.1.call-done = (f32[1024,128]{0,1:T(8,128)}, f32[8192,1024]{0,1:T(8,128)}) async-done(((f32[1024,128]{0,1:T(8,128)}, f32[8192,1024]{0,1:T(8,128)}), (f32[1024,128]{0,1:T(8,128)}, f32[8192,1024]{0,1:T(8,128)})) %all-reduce.3.cloned.1.call-update) | async-done | bytes 34078736 | tf_op jit(solution)/shard_map/psum | solution.py:90
  (327 shorter events, 328.9 us)
Async XLA Ops:
  7.2 244.8 %copy-start.2 = (bf16[512,1024]{1,0:T(8,128)(2,1)S(1)}, bf16[512,1024]{1,0:T(8,128)(2,1)}, u32[]{:S(2)}) copy-start(bf16[512,1024]{1,0:T(8,128)(2,1)} %param.12) | copy-start | bytes 3145732
  7.2 154.8 %all-gather.3.cloned.1.call-start = ((), (), s32[]{:S(2)}) async-start(), calls=%async_computation | async-start | bytes 10485760 | tf_op jit(solution)/shard_map/all_gather | solution.py:67
  7.9 244.0 %all-gather.5.cloned.1.call-start = ((), (), s32[]{:S(2)}) async-start(), calls=%async_computation.1 | async-start | bytes 18874368 | tf_op jit(solution)/shard_map/all_gather | solution.py:79
  8.7 260.7 %copy-start.3 = (bf16[1024,128]{1,0:T(8,128)(2,1)S(1)}, bf16[1024,128]{1,0:T(8,128)(2,1)}, u32[]{:S(2)}) copy-start(bf16[1024,128]{1,0:T(8,128)(2,1)} %param.15) | copy-start | bytes 786436
  8.7 1198.7 %all-reduce.3.cloned.1.call-start = ((), (), s32[]{:S(2)}) async-start(), calls=%async_computation.2 | async-start | bytes 68157440 | tf_op jit(solution)/shard_map/psum | solution.py:90
  268.1 3.4 collective-permute-start.1
  366.8 7.6 collective-permute-start
  465.7 315.1 %copy-start.1 = (f32[512,1024]{1,0:T(8,128)S(1)}, f32[512,1024]{1,0:T(8,128)}, u32[]{:S(2)}) copy-start(f32[512,1024]{1,0:T(8,128)} %get-tuple-element.259) | copy-start | bytes 6291460
  470.2 5.8 copy-start
  489.9 5.8 copy-start
  509.6 5.8 copy-start
  529.3 5.8 copy-start
  549.0 5.8 copy-start
  568.7 5.8 copy-start
  588.4 5.8 copy-start
  608.1 5.8 copy-start
  627.7 5.8 copy-start
  647.4 5.8 copy-start
  667.1 5.8 copy-start
  686.8 5.8 copy-start
  706.5 5.8 copy-start
  726.2 5.8 copy-start
  745.9 5.8 copy-start
  765.6 5.8 copy-start
Sparse Core Ops, SparseCore 0:
  9.6 152.3 all-gather.2
  163.8 88.0 all-gather.4
  798.7 408.6 all-reduce.2
where the time goes:
time: 1230 us
  waiting for transfers between devices  653 us (53%)
  other arithmetic  299 us (24%)
  local copies, waits for them, and re-layouts  206 us (17%)
  matrix products  34 us (3%)
  between operations  13.9 us (1%)
  loops' own time  12.8 us (1%)
    psum x1, waiting for transfers between devices, shards(): grad_filter = lax.psum(local_filter, 'ctx')  406 us
    all_gather x1, waiting for transfers between devices, shards(): gathered = lax.all_gather(cotangent, 'ch', axis=1, tiled=True)  153 us
    reduce_sum x16, other arithmetic, filter_one_group(): return jnp.sum(stacked * gate_f[None], axis=1)  141 us
    add x32, other arithmetic, tap_one_group(): total = total + weights[:, inner][None, :] * slab[begin:begin + tokens]  137 us
    while x144, local copies, waits for them, and re-layouts  135 us
    all_gather x1, waiting for transfers between devices, shards(): lax.all_gather(proj_weight, 'ctx', axis=0, tiled=True)  90 us
    slice x32, local copies, waits for them, and re-layouts, tap_one_group(): total = total + weights[:, inner][None, :] * slab[begin:begin + tokens]  35.9 us
  transfers between devices with their start and end apart: 5, of which 5 were waited for; matrix products, arithmetic and copies ran while one was open for 0% of the time, Pallas kernels for 0%

commit v1 on v0

v1 whole, which is shorter than its diff:
```python
import jax
import jax.numpy as jnp
import numpy as np
from jax import lax
from jax.sharding import PartitionSpec as P

TAPS = 128


def from_behind(x, axis, by):
    length = lax.axis_size(axis)
    pairs = [(i, i + by) for i in range(length) if 0 <= i + by < length]
    return lax.ppermute(x, axis, pairs)


def basis(points):
    freqs = points // 2
    phase = (2 * np.arange(freqs)[:, None] + 1) * np.arange(points)[None, :] % (2 * points)
    angle = np.pi * phase / points
    return np.concatenate([np.cos(angle), np.sin(angle)], 0).astype(np.float32)


def split(a):
    a = jnp.asarray(a, jnp.float32)
    hi = a.astype(jnp.bfloat16)
    return hi, (a - hi.astype(jnp.float32)).astype(jnp.bfloat16)


def dot32(a, b):
    return jnp.dot(a, b, preferred_element_type=jnp.float32)


def forward(table, x):
    hi, lo = split(table)
    return dot32(hi, x) + dot32(lo, x)


def backward(table, y):
    thi, tlo = split(table)
    yhi, ylo = split(y)
    return dot32(thi, yhi) + dot32(thi, ylo) + dot32(tlo, yhi)


def halves(x):
    n = x.shape[0] // 2
    return x[:n], x[n:]


def times(x, f):
    (xc, xs), (fc, fs) = halves(x), halves(f)
    return jnp.concatenate([xc * fc - xs * fs, xc * fs + xs * fc], 0)


def times_conj(x, f):
    (xc, xs), (fc, fs) = halves(x), halves(f)
    return jnp.concatenate([xc * fc + xs * fs, xs * fc - xc * fs], 0)


def shards(query_act, key_act, value_act, filters, proj_weight, cotangent):
    tokens = query_act.shape[0]
    points = tokens + TAPS
    table = basis(points)
    inverse = (table.T / (points // 2)).astype(np.float32)
    gathered = lax.all_gather(cotangent, "ch", axis=1, tiled=True)
    weight = lax.all_gather(proj_weight, "ctx", axis=0, tiled=True)
    query_f = query_act.astype(jnp.float32)
    key_f = key_act.astype(jnp.float32)
    value_f = value_act.astype(jnp.float32)
    product = (key_f * value_f).astype(jnp.bfloat16)
    before = from_behind(product[tokens - TAPS :], "ctx", 1)
    filt_spec = forward(table[:, :TAPS], filters.T)
    prod_spec = forward(table[:, :TAPS], before) + forward(table[:, TAPS:], product)
    mixed = backward(inverse[TAPS:], times(prod_spec, filt_spec))
    gated = (query_f * mixed).astype(jnp.bfloat16)
    partial_grad = lax.dot_general(
        gathered, gated, (((0,), (0,)), ((), ())), preferred_element_type=jnp.float32
    ).astype(jnp.bfloat16)
    grad_proj = lax.psum_scatter(partial_grad, "ctx", scatter_dimension=0, tiled=True).astype(
        jnp.float32
    )
    grad_mix = dot32(gathered, weight)
    grad_query = (grad_mix * mixed).astype(jnp.bfloat16)
    grad_gate = (grad_mix * query_f).astype(jnp.bfloat16)
    after = from_behind(grad_gate[:TAPS], "ctx", -1)
    own_spec = forward(table[:, :tokens], grad_gate)
    gate_spec = own_spec + forward(table[:, tokens:], after)
    lags = inverse[TAPS - np.arange(TAPS)]
    local_filter = backward(lags, times_conj(prod_spec, own_spec))
    grad_filter = lax.psum(local_filter, "ctx").T
    grad_prod = backward(inverse[:tokens], times_conj(gate_spec, filt_spec))
    grad_key = (grad_prod * value_f).astype(jnp.bfloat16)
    grad_value = (grad_prod * key_f).astype(jnp.bfloat16)
    return (grad_query, grad_key, grad_value, grad_filter, grad_proj)


def solution(mesh):
    return jax.shard_map(
        shards,
        mesh=mesh,
        in_specs=(
            P("ctx", "ch"),
            P("ctx", "ch"),
            P("ctx", "ch"),
            P("ch", None),
            P("ctx", "ch"),
            P("ctx", "ch"),
        ),
        out_specs=(P("ctx", "ch"), P("ctx", "ch"), P("ctx", "ch"), P("ch", None), P("ctx", "ch")),
        check_vma=False,
    )
```

time: 1230 us -> 498 us (0.40)
  other arithmetic: 299 us -> 3.06 us
  waiting for transfers between devices: 653 us -> 407 us
  local copies, waits for them, and re-layouts: 206 us -> 15.9 us
  matrix products: 34 us -> 48.7 us
  loops' own time: 12.8 us -> 0 us
    psum x1, waiting for transfers between devices: 406 us -> 53.9 us  [shards(): grad_filter = lax.psum(local_filter, 'ctx').T]
    reduce_sum x16 -> x0, other arithmetic: 141 us -> none  [filter_one_group(): return jnp.sum(stacked * gate_f[None], axis=1)]
    while x144 -> x0, local copies, waits for them, and re-layouts: 135 us -> none
    add x32 -> x2, other arithmetic: 137 us -> 3.06 us  [times_conj(): return jnp.concatenate([xc * fc + xs * fs, xs * fc - xc * fs], 0)]
    reduce_scatter x0 -> x1, waiting for transfers between devices: none -> 111 us  [shards(): lax.psum_scatter(partial_grad, 'ctx', scatter_dimension=0, tiled=True)]
    slice x34 -> x2, local copies, waits for them, and re-layouts: 36 us -> 0.05 us  [the longest x1 0.03 us: shards(): before = from_behind(product[tokens - TAPS:], 'ctx', 1)]
    convert_element_type x51 -> x0, other arithmetic: 20.6 us -> none  [the longest x32 7.67 us: tap_one_group(): lax.dynamic_slice_in_dim(extended, first, tokens + group_width - 1, 0)]
    dot_general x1 -> x20, matrix products: 16.1 us -> 32.9 us  [dot32(): return jnp.dot(a, b, preferred_element_type=jnp.float32)]
  transfers between devices with their start and end apart: 5 -> 6, of which waited for: 5 -> 5; matrix products, arithmetic and copies ran while one was open for 0% -> 4% of each run, Pallas kernels for 0% -> 0%
where the time goes in v1:
time: 498 us; the launch traced here: 497 us
  waiting for transfers between devices  407 us (82%)
  matrix products  48.7 us (10%)
  local copies, waits for them, and re-layouts  15.9 us (3%)
  between operations  14.1 us (3%)
  starting transfers between devices  8.5 us (2%)
    all_gather x1, waiting for transfers between devices, shards(): gathered = lax.all_gather(cotangent, 'ch', axis=1, tiled=True)  150 us
    reduce_scatter x1, waiting for transfers between devices, shards(): lax.psum_scatter(partial_grad, 'ctx', scatter_dimension=0, tiled=True)  111 us
    all_gather x1, waiting for transfers between devices, shards(): weight = lax.all_gather(proj_weight, 'ctx', axis=0, tiled=True)  90 us
    psum x1, waiting for transfers between devices, shards(): grad_filter = lax.psum(local_filter, 'ctx').T  53.9 us
    dot_general x20, matrix products, dot32(): return jnp.dot(a, b, preferred_element_type=jnp.float32)  32.9 us
    dot_general x1, matrix products, shards(): lax.dot_general(gathered, gated, (((0,), (0,)), ((), ())), preferred_elem...  15.9 us
    unnamed x58, local copies, waits for them, and re-layouts  15.9 us
  transfers between devices with their start and end apart: 6, of which 5 were waited for; matrix products, arithmetic and copies ran while one was open for 4% of the time, Pallas kernels for 0%

profile of v1, /device:TPU:0, one launch (start us, length us, event | category | flops | bytes accessed | tf_op | source)
XLA Modules:
  0.0 497.0 jit_solution(8108205557831197759)
XLA Ops:
  7.2 0.7 all-gather.3.cloned.1.call-update
  8.0 0.7 all-gather.5.cloned.1.call-update
  8.8 1.3 copy.19
  10.1 1.3 copy.20
  12.4 149.5 %all-gather.3.cloned.1.call-done = bf16[512,8192]{1,0:T(8,128)(2,1)} async-done(((bf16[512,2048]{1,0:T(8,128)(2,1)}), bf16[512,8192]{1,0:T(8,128)(2,1)}) %all-gather.3.cloned.1.call-update) | async-done | bytes 8388624 | tf_op jit(solution)/shard_map/all_gather | solution.py:64
  162.0 90.0 %all-gather.5.cloned.1.call-done = bf16[8192,1024]{1,0:T(8,128)(2,1)} async-done(((bf16[1024,1024]{1,0:T(8,128)(2,1)}), bf16[8192,1024]{1,0:T(8,128)(2,1)}) %all-gather.5.cloned.1.call-update) | async-done | bytes 16777232 | tf_op jit(solution)/shard_map/all_gather | solution.py:65
  251.9 14.9 %fusion.6 = (bf16[512,1024]{1,0:T(8,128)(2,1)S(1)}, f32[512,1024]{1,0:T(8,128)S(1)}) fusion(bf16[512,1024]{1,0:T(8,128)(2,1)} %param.14, bf16[512,8192]{1,0:T(8,128)(2,1)} %all-gather.3.cloned.1.call-done, bf16[8192,1024]{1,0:T(8,128)(2,1)} %all-gather.5.cloned.1.call-done), kind=kOutput, calls=%fused_computation.20 | convolution fusion | flops 8591507456 | bytes 29360128 | tf_op jit(solution)/shard_map/dot_general | solution.py:30
  266.9 1.4 collective-permute-start.1
  268.4 0.9 fusion.40
  269.2 0.9 convolution_add_fusion.1
  271.5 0.6 multiply_add_fusion.1
  272.6 1.0 fusion.8
  273.7 1.0 fusion.21
  275.4 2.7 fusion.3
  278.1 6.7 %collective-permute-start = (bf16[128,1024]{0,1:T(8,128)(2,1)S(1)}, bf16[128,1024]{0,1:T(8,128)(2,1)S(1)}, u32[]{:S(2)}, u32[]{:S(2)}) collective-permute-start(bf16[128,1024]{0,1:T(8,128)(2,1)S(1)} %slice.44), channel_id=1, source_target_pairs={{0,4},{4,8},{8,12},{12,16},{16,20},{20,24},{24,28},{1,5},{5,9},{9,... | collective-permute-start | bytes 786440 | tf_op jit(solution)/shard_map/ppermute | solution.py:13
  284.8 0.9 fusion.38
  285.7 0.9 fusion.37
  287.5 0.7 add_add_fusion.1
  288.2 2.5 multiply_add_fusion
  290.7 1.0 fusion.14
  291.8 1.0 fusion.17
  292.8 2.1 multiply_convert_fusion
  294.9 15.9 %convert_bitcast_fusion = bf16[8192,1024]{0,1:T(8,128)(2,1)} fusion(bf16[512,8192]{1,0:T(8,128)(2,1)} %all-gather.3.cloned.1.call-done, f32[512,1024]{1,0:T(8,128)S(1)} %get-tuple-element.24, bf16[512,1024]{1,0:T(8,128)(2,1)S(1)} %copy-done.25), kind=kOutput, calls=%fused_computation | convolution fusion | flops 8599896064 | bytes 28311552 | tf_op jit(solution)/shard_map/dot_general | solution.py:75
  311.0 1.0 copy-done.2
  313.0 0.5 fusion.11
  313.9 1.4 fusion.12
  315.4 2.4 copy.26
  317.7 1.3 copy.25
  319.0 111.5 %reduce-scatter.2.cloned.1.call-done = bf16[1024,1024]{0,1:T(8,128)(2,1)} async-done(((bf16[8192,1024]{0,1:T(8,128)(2,1)}), bf16[1024,1024]{0,1:T(8,128)(2,1)}) %reduce-scatter.2.cloned.1.call-update) | async-done | bytes 2097168 | tf_op jit(solution)/shard_map/reduce_scatter | solution.py:78
  430.5 4.2 copy.27
  434.6 53.9 %all-reduce.2.cloned.1.call-done = f32[1024,128]{1,0:T(8,128)} async-done(((f32[1024,128]{1,0:T(8,128)}), f32[1024,128]{1,0:T(8,128)}) %all-reduce.2.cloned.1.call-update) | async-done | bytes 524304 | tf_op jit(solution)/shard_map/psum | solution.py:89
  488.6 1.9 copy.33
  (67 shorter events, 6.4 us)
Async XLA Ops:
  7.2 4.2 copy-start
  7.2 1.6 copy-start.10
  7.2 154.8 %all-gather.3.cloned.1.call-start = ((), (), s32[]{:S(2)}) async-start(), calls=%async_computation.1 | async-start | bytes 10485760 | tf_op jit(solution)/shard_map/all_gather | solution.py:64
  7.9 2.2 copy-start.11
  7.9 244.0 %all-gather.5.cloned.1.call-start = ((), (), s32[]{:S(2)}) async-start(), calls=%async_computation.2 | async-start | bytes 18874368 | tf_op jit(solution)/shard_map/all_gather | solution.py:65
  8.7 2.7 copy-start.20
  8.7 421.8 %reduce-scatter.2.cloned.1.call-start = ((), (), s32[]{:S(2)}) async-start(), calls=%async_computation.4 | async-start | bytes 18874368 | tf_op jit(solution)/shard_map/reduce_scatter | solution.py:78
  10.1 1.8 copy-start.13
  12.4 255.9 %copy-start.9 = (bf16[640,512]{1,0:T(8,128)(2,1)S(1)}, bf16[640,512]{1,0:T(8,128)(2,1)}, u32[]{:S(2)}) copy-start(bf16[640,512]{1,0:T(8,128)(2,1)} %constant.33) | copy-start | bytes 1966084
  266.9 2.3 copy-start.18
  266.9 3.6 collective-permute-start.1
  269.2 1.2 copy-start.22
  270.1 0.9 copy-start.24
  271.5 1.1 copy-start.8
  273.7 1.2 copy-start.5
  273.7 1.5 copy-start.6
  273.7 1.7 copy-start.12
  275.4 9.4 %copy-start.17 = (bf16[640,512]{1,0:T(8,128)(2,1)S(1)}, bf16[640,512]{1,0:T(8,128)(2,1)}, u32[]{:S(2)}) copy-start(bf16[640,512]{1,0:T(8,128)(2,1)} %constant.28) | copy-start | bytes 1966084
  278.1 7.6 %copy-start.16 = (bf16[640,512]{1,0:T(8,128)(2,1)S(1)}, bf16[640,512]{1,0:T(8,128)(2,1)}, u32[]{:S(2)}) copy-start(bf16[640,512]{1,0:T(8,128)(2,1)} %constant.25) | copy-start | bytes 1966084
  278.1 8.5 %collective-permute-start = (bf16[128,1024]{0,1:T(8,128)(2,1)S(1)}, bf16[128,1024]{0,1:T(8,128)(2,1)S(1)}, u32[]{:S(2)}, u32[]{:S(2)}) collective-permute-start(bf16[128,1024]{0,1:T(8,128)(2,1)S(1)} %slice.44), channel_id=1, source_target_pairs={{0,4},{4,8},{8,12},{12,16},{16,20},{20,24},{24,28},{1,5},{5,9},{9,... | collective-permute-start | bytes 786440 | tf_op jit(solution)/shard_map/ppermute | solution.py:13
  285.7 0.9 copy-start.14
  286.6 0.9 copy-start.21
  288.2 2.5 copy-start.15
  290.7 1.1 copy-start.7
  292.7 2.1 copy-start.25
  310.7 1.3 copy-start.2
  310.7 1.7 copy-start.3
  310.7 1.7 copy-start.19
  310.8 177.8 %all-reduce.2.cloned.1.call-start = ((), (), s32[]{:S(2)}) async-start(), calls=%async_computation.3 | async-start | bytes 1048576 | tf_op jit(solution)/shard_map/psum | solution.py:89
  313.0 0.9 copy-start.23
  315.3 2.4 copy-start.4
  430.5 60.0 %copy-start.1 = (bf16[1024,128]{1,0:T(8,128)(2,1)S(1)}, bf16[1024,128]{1,0:T(8,128)(2,1)}, u32[]{:S(2)}) copy-start(bf16[1024,128]{1,0:T(8,128)(2,1)} %param.17) | copy-start | bytes 786436
Sparse Core Ops, SparseCore 0:
  9.6 152.3 all-gather.2
  163.9 88.0 all-gather.4
  310.9 119.5 reduce-scatter.1
  434.0 54.5 all-reduce.1

commit v2 on v1

--- a/solution.py
+++ b/solution.py
@@ -1,7 +1,11 @@
+import functools
+
 import jax
 import jax.numpy as jnp
 import numpy as np
 from jax import lax
+from jax.experimental import pallas as pl
+from jax.experimental.pallas import tpu as pltpu
 from jax.sharding import PartitionSpec as P
 
 TAPS = 128
@@ -56,13 +60,244 @@
     return jnp.concatenate([xc * fc + xs * fs, xs * fc - xc * fs], 0)
 
 
+MESH = pl.DeviceIdType.MESH
+CHUNKS = 4
+
+
+def exchange_kernel(n_ctx, n_ch, cot, weight, gated, grad_mix, grad_proj, blocks, weights, mine,
+                    partner_out, partner_in, arrived, own_sem, z_send, z_recv, w_send, w_recv,
+                    f_send, f_recv, p_send, p_recv, r_send, r_recv):
+    chips = n_ctx // 2
+    per = n_ctx // n_ch
+    hops = n_ch - 1
+    ctx = lax.axis_index("ctx")
+    ch = lax.axis_index("ch")
+    chip, core = ctx // 2, ctx % 2
+    other = chip * 2 + 1 - core
+    rows = weight.shape[0]
+    wide = rows // CHUNKS
+
+    def chip_at(off):
+        return (chip + off) % chips
+
+    barrier = pltpu.get_barrier_semaphore()
+    for off in range(1, n_ctx):
+        pl.semaphore_signal(barrier, inc=1, device_id=((ctx + off) % n_ctx, ch), device_id_type=MESH)
+    for off in (1, n_ch - 1):
+        pl.semaphore_signal(barrier, inc=1, device_id=(ctx, (ch + off) % n_ch), device_id_type=MESH)
+
+    def own_copy(s, e):
+        return pltpu.make_async_copy(
+            cot.at[:, pl.ds(e * rows + s * wide, wide)], blocks.at[ch, s, e], own_sem.at[s, e]
+        )
+
+    own_weight = pltpu.make_async_copy(weight, weights.at[ctx], own_sem.at[CHUNKS, 0])
+    for s in range(CHUNKS):
+        for e in range(per):
+            own_copy(s, e).start()
+    own_weight.start()
+    pl.semaphore_wait(barrier, n_ctx + 1)
+
+    def w_copy(off):
+        return pltpu.make_async_remote_copy(
+            weight, weights.at[ctx], w_send.at[off], w_recv.at[off],
+            device_id=(chip_at(off) * 2 + core, ch), device_id_type=MESH)
+
+    def f_copy(off):
+        owner = chip_at(chips - off) * 2 + core
+        return pltpu.make_async_remote_copy(
+            weights.at[owner], weights.at[owner], f_send.at[off], f_recv.at[off],
+            device_id=(other, ch), device_id_type=MESH)
+
+    def z_copy(s, h, way):
+        if way == 0:
+            block, to = ch - h, ch + 1
+        else:
+            block, to = ch + h, ch - 1
+        block = jnp.clip(block, 0, n_ch - 1)
+        return pltpu.make_async_remote_copy(
+            blocks.at[block, s], blocks.at[block, s], z_send.at[s, h, way], z_recv.at[s, h, way],
+            device_id=(ctx, jnp.clip(to, 0, n_ch - 1)), device_id_type=MESH)
+
+    def sends(h, way):
+        if way == 0:
+            return jnp.logical_and(ch >= h, ch < n_ch - 1)
+        return jnp.logical_and(ch + h < n_ch, ch > 0)
+
+    def receives(h, way):
+        if way == 0:
+            return ch - 1 - h >= 0
+        return ch + 1 + h < n_ch
+
+    def p_copy(s, k):
+        return pltpu.make_async_remote_copy(
+            partner_out.at[s % 2, k], partner_in.at[s, k], p_send.at[s, k], p_recv.at[s, k],
+            device_id=(other, ch), device_id_type=MESH)
+
+    def r_copy(s, off):
+        return pltpu.make_async_remote_copy(
+            partner_in.at[s, chip_at(off)], arrived.at[s, off], r_send.at[s, off],
+            r_recv.at[s, off], device_id=(chip_at(off) * 2 + core, ch), device_id_type=MESH)
+
+    def partial_sum(s, k, e):
+        target = k * 2 + e
+        return lax.dot_general(
+            blocks[target // per, s, target % per], gated[...], (((0,), (0,)), ((), ())),
+            preferred_element_type=jnp.float32)
+
+    def reduce_chunk(s):
+        @pl.loop(0, chips)
+        def _(k):
+            if s >= 2:
+                p_copy(s - 2, k).wait_send()
+            partner_out[s % 2, k] = partial_sum(s, k, 1 - core).astype(jnp.bfloat16)
+            p_copy(s, k).start()
+
+        @pl.loop(0, chips)
+        def _(k):
+            mine[k] = partial_sum(s, k, core)
+
+        @pl.loop(1, chips)
+        def _(off):
+            k = chip_at(off)
+            p_copy(s, k).wait_recv()
+            partner_in[s, k] = (mine[k] + partner_in[s, k].astype(jnp.float32)).astype(jnp.bfloat16)
+            r_copy(s, off).start()
+
+        p_copy(s, chip).wait_recv()
+        grad_proj[pl.ds(s * wide, wide), :] = mine[chip] + partner_in[s, chip].astype(jnp.float32)
+
+    def finish_chunk(s):
+        @pl.loop(1, chips)
+        def _(off):
+            r_copy(s, off).wait_recv()
+            grad_proj[pl.ds(s * wide, wide), :] += arrived[s, off].astype(jnp.float32)
+
+    for stage in range(CHUNKS + hops - 1):
+        if stage < CHUNKS:
+            for e in range(per):
+                own_copy(stage, e).wait()
+        for h in reversed(range(hops)):
+            s = stage - h
+            if 0 <= s < CHUNKS:
+                for way in range(2):
+                    @pl.when(sends(h, way))
+                    def _():
+                        z_copy(s, h, way).start()
+        if stage == 0:
+            @pl.loop(1, chips)
+            def _(off):
+                w_copy(off).start()
+            own_weight.wait()
+            f_copy(0).start()
+        if stage >= hops:
+            reduce_chunk(stage - hops)
+        for h in range(hops):
+            s = stage - h
+            if 0 <= s < CHUNKS:
+                for way in range(2):
+                    @pl.when(receives(h, way))
+                    def _():
+                        z_copy(s, h, way).wait_recv()
+        if stage == hops - 1:
+            @pl.loop(1, chips)
+            def _(off):
+                w_copy(off).wait_recv()
+                f_copy(off).start()
+    reduce_chunk(CHUNKS - 1)
+
+    @pl.loop(0, chips)
+    def _(off):
+        f_copy(off).wait_recv()
+
+    grad_mix[...] = jnp.zeros_like(grad_mix)
+
+    @pl.loop(0, n_ctx)
+    def _(i):
+        total = grad_mix[...]
+        for s in range(CHUNKS):
+            total += jnp.dot(
+                blocks[i // per, s, i % per], weights[i, pl.ds(s * wide, wide), :],
+                preferred_element_type=jnp.float32)
+        grad_mix[...] = total
+
+    for s in range(CHUNKS):
+        finish_chunk(s)
+
+    for s in range(CHUNKS):
+        for h in range(hops):
+            for way in range(2):
+                @pl.when(sends(h, way))
+                def _():
+                    z_copy(s, h, way).wait_send()
+
+        @pl.loop(1, chips)
+        def _(off):
+            r_copy(s, off).wait_send()
+
+        if s >= CHUNKS - 2:
+            @pl.loop(0, chips)
+            def _(k):
+                p_copy(s, k).wait_send()
+
+    @pl.loop(1, chips)
+    def _(off):
+        w_copy(off).wait_send()
+
+    @pl.loop(0, chips)
+    def _(off):
+        f_copy(off).wait_send()
+
+
+def exchange(cotangent, proj_weight, gated):
+    n_ctx, n_ch = lax.axis_size("ctx"), lax.axis_size("ch")
+    tokens, channels = gated.shape
+    rows = proj_weight.shape[0]
+    wide = rows // CHUNKS
+    chips, per, hops = n_ctx // 2, n_ctx // n_ch, n_ch - 1
+    dma = pltpu.SemaphoreType.DMA
+    return pl.pallas_call(
+        functools.partial(exchange_kernel, n_ctx, n_ch),
+        out_shape=(
+            jax.ShapeDtypeStruct((tokens, channels), jnp.float32),
+            jax.ShapeDtypeStruct((rows, channels), jnp.float32),
+        ),
+        in_specs=[
+            pl.BlockSpec(memory_space=pl.ANY),
+            pl.BlockSpec(memory_space=pl.ANY),
+            pl.BlockSpec(memory_space=pltpu.VMEM),
+        ],
+        out_specs=[pl.BlockSpec(memory_space=pltpu.VMEM)] * 2,
+        scratch_shapes=[
+            pltpu.VMEM((n_ch, CHUNKS, per, tokens, wide), jnp.bfloat16),
+            pltpu.VMEM((n_ctx, rows, channels), jnp.bfloat16),
+            pltpu.VMEM((chips, wide, channels), jnp.float32),
+            pltpu.VMEM((2, chips, wide, channels), jnp.bfloat16),
+            pltpu.VMEM((CHUNKS, chips, wide, channels), jnp.bfloat16),
+            pltpu.VMEM((CHUNKS, chips, wide, channels), jnp.bfloat16),
+            dma((CHUNKS + 1, per)),
+            dma((CHUNKS, hops, 2)),
+            dma((CHUNKS, hops, 2)),
+            dma((chips,)),
+            dma((chips,)),
+            dma((chips,)),
+            dma((chips,)),
+            dma((CHUNKS, chips)),
+            dma((CHUNKS, chips)),
+            dma((CHUNKS, chips)),
+            dma((CHUNKS, chips)),
+        ],
+        compiler_params=pltpu.CompilerParams(
+            collective_id=0, has_side_effects=True, vmem_limit_bytes=62 * 2**20
+        ),
+    )(cotangent, proj_weight, gated)
+
+
 def shards(query_act, key_act, value_act, filters, proj_weight, cotangent):
     tokens = query_act.shape[0]
     points = tokens + TAPS
     table = basis(points)
     inverse = (table.T / (points // 2)).astype(np.float32)
-    gathered = lax.all_gather(cotangent, "ch", axis=1, tiled=True)
-    weight = lax.all_gather(proj_weight, "ctx", axis=0, tiled=True)
     query_f = query_act.astype(jnp.float32)
     key_f = key_act.astype(jnp.float32)
     value_f = value_act.astype(jnp.float32)
@@ -72,13 +307,7 @@
     prod_spec = forward(table[:, :TAPS], before) + forward(table[:, TAPS:], product)
     mixed = backward(inverse[TAPS:], times(prod_spec, filt_spec))
     gated = (query_f * mixed).astype(jnp.bfloat16)
-    partial_grad = lax.dot_general(
-        gathered, gated, (((0,), (0,)), ((), ())), preferred_element_type=jnp.float32
-    ).astype(jnp.bfloat16)
-    grad_proj = lax.psum_scatter(partial_grad, "ctx", scatter_dimension=0, tiled=True).astype(
-        jnp.float32
-    )
-    grad_mix = dot32(gathered, weight)
+    grad_mix, grad_proj = exchange(cotangent, proj_weight, gated)
     grad_query = (grad_mix * mixed).astype(jnp.bfloat16)
     grad_gate = (grad_mix * query_f).astype(jnp.bfloat16)
     after = from_behind(grad_gate[:TAPS], "ctx", -1)

time: 498 us -> 319 us (0.64)
  waiting for transfers between devices: 407 us -> 45.6 us
  Pallas kernels: 0 us -> 213 us
  matrix products: 48.7 us -> 17.3 us
    all_gather x2 -> x0, waiting for transfers between devices: 239 us -> none  [the longest x1 150 us: shards(): gathered = lax.all_gather(cotangent, 'ch', axis=1, tiled=True)]
    pallas_call x0 -> x1, Pallas kernels: none -> 213 us  [exchange(): pl.pallas_call(functools.partial(exchange_kernel, n_ctx, n_ch), out_shape...]
    reduce_scatter x1 -> x0, waiting for transfers between devices: 111 us -> none  [shards(): lax.psum_scatter(partial_grad, 'ctx', scatter_dimension=0, tiled=True)]
    dot_general x1 -> x0, matrix products: 15.9 us -> none  [shards(): lax.dot_general(gathered, gated, (((0,), (0,)), ((), ())), preferred_elem...]
    dot_general x20 -> x19, matrix products: 32.9 us -> 17.3 us  [dot32(): return jnp.dot(a, b, preferred_element_type=jnp.float32)]
    psum x1, waiting for transfers between devices: 53.9 us -> 45.6 us  [shards(): grad_filter = lax.psum(local_filter, 'ctx').T]
  transfers between devices with their start and end apart: 6 -> 3, of which waited for: 5 -> 1; matrix products, arithmetic and copies ran while one was open for 4% -> 4% of each run, Pallas kernels for 0% -> 0%
where the time goes in v2:
time: 319 us
  Pallas kernels  213 us (67%)
  waiting for transfers between devices  45.6 us (14%)
  local copies, waits for them, and re-layouts  17.7 us (6%)
  matrix products  17.3 us (5%)
  between operations  14.4 us (5%)
  other arithmetic  6.48 us (2%)
  starting transfers between devices  4.05 us (1%)
    pallas_call x1, Pallas kernels, exchange(): pl.pallas_call(functools.partial(exchange_kernel, n_ctx, n_ch), out_shape...  213 us
    psum x1, waiting for transfers between devices, shards(): grad_filter = lax.psum(local_filter, 'ctx').T  45.6 us
    unnamed x58, local copies, waits for them, and re-layouts  17.7 us
    dot_general x19, matrix products, dot32(): return jnp.dot(a, b, preferred_element_type=jnp.float32)  17.3 us
  transfers between devices with their start and end apart: 3, of which 1 were waited for; matrix products, arithmetic and copies ran while one was open for 4% of the time, Pallas kernels for 0%

profile of v2, /device:TPU:0, one launch (start us, length us, event | category | flops | bytes accessed | tf_op | source)
XLA Modules:
  0.0 318.7 jit_solution(3151151990068935105)
XLA Ops:
  7.2 1.6 copy.19
  9.9 2.5 collective-permute-start
  12.4 0.9 fusion.36
  14.7 0.6 copy-done.20
  15.3 0.9 fusion.37
  16.7 0.7 add_add_fusion.1
  17.4 0.8 multiply_subtract_fusion.2
  18.3 0.9 copy-done.4
  19.2 1.0 fusion.16
  20.3 1.0 fusion.13
  21.5 2.7 fusion.3
  24.2 213.1 %shard_map.173 = (f32[512,1024]{1,0:T(8,128)}, f32[1024,1024]{1,0:T(8,128)}) custom-call(bf16[512,2048]{1,0:T(8,128)(2,1)} %cot.1, bf16[1024,1024]{1,0:T(8,128)(2,1)} %weight.1, bf16[512,1024]{1,0:T(8,128)(2,1)} %get-tuple-element.24.gated), custom_call_target="tpu_custom_call" | custom-call | tf_op jit(solution)/shard_map/pallas_call | solution.py:259
  237.3 3.9 %fusion.4 = (bf16[512,1024]{1,0:T(8,128)(2,1)S(1)}, bf16[512,1024]{1,0:T(8,128)(2,1)}) fusion(f32[512,1024]{1,0:T(8,128)} %get-tuple-element.7, bf16[512,1024]{1,0:T(8,128)(2,1)S(1)} %copy-done.10, f32[512,1024]{1,0:T(8,128)} %get-tuple-element.25), kind=kLoop, calls=%fused_computation.17 | loop fusion | flops 2621440 | bytes 7340032 | tf_op jit(solution)/shard_map/convert_element_type | solution.py:312
  241.3 0.8 fusion.39
  242.4 0.9 convolution_add_fusion.1
  243.3 0.9 copy-done.5
  244.2 0.6 multiply_add_fusion
  244.7 1.5 collective-permute-start.1
  246.3 0.6 fusion.24
  246.8 0.6 fusion.11
  247.7 1.4 fusion.12
  250.1 0.6 add_add_fusion
  250.7 1.2 copy-done.3
  251.8 0.8 multiply_add_fusion.1
  252.9 1.1 fusion.8
  254.0 1.0 fusion.20
  255.7 1.2 fusion.5
  256.9 1.3 copy.25
  258.2 1.3 copy.26
  259.6 45.6 %all-reduce.2.cloned.1.call-done = f32[1024,128]{1,0:T(8,128)} async-done(((f32[1024,128]{1,0:T(8,128)}), f32[1024,128]{1,0:T(8,128)}) %all-reduce.2.cloned.1.call-update) | async-done | bytes 524304 | tf_op jit(solution)/shard_map/psum | solution.py:318
  305.1 1.9 copy.33
  307.0 4.8 %copy.34 = f32[1024,1024]{1,0:T(8,128)} copy(f32[1024,1024]{1,0:T(8,128)} %get-tuple-element.35) | data formatting | bytes 8388608
  (60 shorter events, 5.7 us)
Async XLA Ops:
  7.2 6.1 %copy-start = (bf16[1024,128]{1,0:T(8,128)(2,1)S(1)}, bf16[1024,128]{1,0:T(8,128)(2,1)}, u32[]{:S(2)}) copy-start(bf16[1024,128]{1,0:T(8,128)(2,1)} %param.17) | copy-start | bytes 786436
  7.2 1.7 copy-start.14
  7.2 297.9 %all-reduce.2.cloned.1.call-start = ((), (), s32[]{:S(2)}) async-start(), calls=%async_computation | async-start | bytes 1048576 | tf_op jit(solution)/shard_map/psum | solution.py:318
  8.8 1.0 copy-start.6
  9.4 3.9 %copy-start.8 = (bf16[512,1024]{0,1:T(8,128)(2,1)}, bf16[512,1024]{0,1:T(8,128)(2,1)S(1)}, u32[]{:S(2)}) copy-start(bf16[512,1024]{0,1:T(8,128)(2,1)S(1)} %copy.20) | copy-start | bytes 3145732
  9.4 3.0 copy-start.19
  9.9 3.4 %copy-start.22 = (bf16[640,128]{1,0:T(8,128)(2,1)S(1)}, bf16[640,128]{1,0:T(8,128)(2,1)}, u32[]{:S(2)}) copy-start(bf16[640,128]{1,0:T(8,128)(2,1)} %constant.21) | copy-start | bytes 491524
  9.9 6.3 %collective-permute-start = (bf16[128,1024]{0,1:T(8,128)(2,1)S(1)}, bf16[128,1024]{0,1:T(8,128)(2,1)S(1)}, u32[]{:S(2)}, u32[]{:S(2)}) collective-permute-start(bf16[128,1024]{0,1:T(8,128)(2,1)S(1)} %slice.44), channel_id=1, source_target_pairs={{0,4},{4,8},{8,12},{12,16},{16,20},{20,24},{24,28},{1,5},{5,9},{9,... | collective-permute-start | bytes 786440 | tf_op jit(solution)/shard_map/ppermute | solution.py:17
  13.3 0.9 copy-start.16
  14.2 1.1 copy-start.20
  15.3 2.1 copy-start.2
  17.4 1.8 copy-start.4
  17.4 1.7 copy-start.11
  19.2 1.1 copy-start.18
  20.3 1.2 copy-start.10
  237.3 4.0 %copy-start.13 = (bf16[640,512]{1,0:T(8,128)(2,1)S(1)}, bf16[640,512]{1,0:T(8,128)(2,1)}, u32[]{:S(2)}) copy-start(bf16[640,512]{1,0:T(8,128)(2,1)} %constant.33) | copy-start | bytes 1966084
  241.3 1.1 copy-start.17
  242.4 1.7 copy-start.5
  244.2 2.1 copy-start.21
  244.7 4.5 %collective-permute-start.1 = (bf16[128,1024]{1,0:T(8,128)(2,1)S(1)}, bf16[128,1024]{1,0:T(8,128)(2,1)S(1)}, u32[]{:S(2)}, u32[]{:S(2)}) collective-permute-start(bf16[128,1024]{1,0:T(8,128)(2,1)S(1)} %slice.49), channel_id=1, source_target_pairs={{4,0},{8,4},{12,8},{16,12},{20,16},{24,20},{28,24},{5,1},{9,5},{13... | collective-permute-start | bytes 786440 | tf_op jit(solution)/shard_map/ppermute | solution.py:17
  246.8 0.9 copy-start.25
  247.7 1.5 copy-start.23
  249.2 0.9 copy-start.24
  250.1 1.7 copy-start.3
  251.8 1.1 copy-start.12
  254.0 1.2 copy-start.7
  254.0 1.5 copy-start.9
  254.0 1.7 copy-start.15
  307.0 4.8 %copy-start.1 = (bf16[1024,128]{1,0:T(8,128)(2,1)S(1)}, bf16[1024,128]{1,0:T(8,128)(2,1)}, u32[]{:S(2)}) copy-start(bf16[1024,128]{1,0:T(8,128)(2,1)} %param.17) | copy-start | bytes 786436
Sparse Core Ops, SparseCore 0:
  249.3 55.7 all-reduce.1

commit v3 on v2

--- a/solution.py
+++ b/solution.py
@@ -64,9 +64,9 @@
 CHUNKS = 4
 
 
-def exchange_kernel(n_ctx, n_ch, cot, weight, gated, grad_mix, grad_proj, blocks, weights, mine,
+def exchange_kernel(n_ctx, n_ch, cot, weight, gated, query, grad_mix, gate, after, grad_proj, blocks, weights, mine,
                     partner_out, partner_in, arrived, own_sem, z_send, z_recv, w_send, w_recv,
-                    f_send, f_recv, p_send, p_recv, r_send, r_recv):
+                    f_send, f_recv, p_send, p_recv, r_send, r_recv, h_sem):
     chips = n_ctx // 2
     per = n_ctx // n_ch
     hops = n_ch - 1
@@ -136,8 +136,26 @@
 
     def r_copy(s, off):
         return pltpu.make_async_remote_copy(
-            partner_in.at[s, chip_at(off)], arrived.at[s, off], r_send.at[s, off],
+            partner_in.at[s, chip_at(off)], arrived.at[s, off - 1], r_send.at[s, off],
             r_recv.at[s, off], device_id=(chip_at(off) * 2 + core, ch), device_id_type=MESH)
+
+    halo_copy = pltpu.make_async_remote_copy(
+        gate.at[pl.ds(0, TAPS)], after, h_sem.at[0], h_sem.at[1],
+        device_id=(jnp.maximum(ctx - 1, 0), ch), device_id_type=MESH)
+
+    def mix_chunk(s):
+        if s == 0:
+            @pl.loop(0, chips)
+            def _(off):
+                f_copy(off).wait_recv()
+
+            grad_mix[...] = jnp.zeros_like(grad_mix)
+
+        @pl.loop(0, n_ctx)
+        def _(i):
+            grad_mix[...] += jnp.dot(
+                blocks[i // per, s, i % per], weights[i, pl.ds(s * wide, wide), :],
+                preferred_element_type=jnp.float32)
 
     def partial_sum(s, k, e):
         target = k * 2 + e
@@ -171,14 +189,15 @@
         @pl.loop(1, chips)
         def _(off):
             r_copy(s, off).wait_recv()
-            grad_proj[pl.ds(s * wide, wide), :] += arrived[s, off].astype(jnp.float32)
+            grad_proj[pl.ds(s * wide, wide), :] += arrived[s, off - 1].astype(jnp.float32)
 
     for stage in range(CHUNKS + hops - 1):
-        if stage < CHUNKS:
+        fresh = [s for s in ((0, 1) if stage == 0 else (stage + 1,)) if s < CHUNKS]
+        for s in fresh:
             for e in range(per):
-                own_copy(stage, e).wait()
-        for h in reversed(range(hops)):
-            s = stage - h
+                own_copy(s, e).wait()
+        ready = [(stage - h, h) for h in reversed(range(1, hops))] + [(s, 0) for s in fresh]
+        for s, h in ready:
             if 0 <= s < CHUNKS:
                 for way in range(2):
                     @pl.when(sends(h, way))
@@ -192,6 +211,8 @@
             f_copy(0).start()
         if stage >= hops:
             reduce_chunk(stage - hops)
+        if hops < stage < CHUNKS + hops - 2:
+            mix_chunk(stage - hops - 1)
         for h in range(hops):
             s = stage - h
             if 0 <= s < CHUNKS:
@@ -206,20 +227,17 @@
                 f_copy(off).start()
     reduce_chunk(CHUNKS - 1)
 
-    @pl.loop(0, chips)
-    def _(off):
-        f_copy(off).wait_recv()
-
-    grad_mix[...] = jnp.zeros_like(grad_mix)
-
-    @pl.loop(0, n_ctx)
-    def _(i):
-        total = grad_mix[...]
-        for s in range(CHUNKS):
-            total += jnp.dot(
-                blocks[i // per, s, i % per], weights[i, pl.ds(s * wide, wide), :],
-                preferred_element_type=jnp.float32)
-        grad_mix[...] = total
+    for s in range(CHUNKS - 3, CHUNKS):
+        mix_chunk(s)
+    gate[...] = (grad_mix[...] * query[...].astype(jnp.float32)).astype(jnp.bfloat16)
+
+    @pl.when(ctx > 0)
+    def _():
+        halo_copy.start()
+
+    @pl.when(ctx == n_ctx - 1)
+    def _():
+        after[...] = jnp.zeros_like(after)
 
     for s in range(CHUNKS):
         finish_chunk(s)
@@ -240,6 +258,14 @@
             def _(k):
                 p_copy(s, k).wait_send()
 
+    @pl.when(ctx > 0)
+    def _():
+        halo_copy.wait_send()
+
+    @pl.when(ctx < n_ctx - 1)
+    def _():
+        halo_copy.wait_recv()
+
     @pl.loop(1, chips)
     def _(off):
         w_copy(off).wait_send()
@@ -249,7 +275,7 @@
         f_copy(off).wait_send()
 
 
-def exchange(cotangent, proj_weight, gated):
+def exchange(cotangent, proj_weight, gated, query_act):
     n_ctx, n_ch = lax.axis_size("ctx"), lax.axis_size("ch")
     tokens, channels = gated.shape
     rows = proj_weight.shape[0]
@@ -260,21 +286,24 @@
         functools.partial(exchange_kernel, n_ctx, n_ch),
         out_shape=(
             jax.ShapeDtypeStruct((tokens, channels), jnp.float32),
+            jax.ShapeDtypeStruct((tokens, channels), jnp.bfloat16),
+            jax.ShapeDtypeStruct((TAPS, channels), jnp.bfloat16),
             jax.ShapeDtypeStruct((rows, channels), jnp.float32),
         ),
         in_specs=[
             pl.BlockSpec(memory_space=pl.ANY),
             pl.BlockSpec(memory_space=pl.ANY),
             pl.BlockSpec(memory_space=pltpu.VMEM),
+            pl.BlockSpec(memory_space=pltpu.VMEM),
         ],
-        out_specs=[pl.BlockSpec(memory_space=pltpu.VMEM)] * 2,
+        out_specs=[pl.BlockSpec(memory_space=pltpu.VMEM)] * 4,
         scratch_shapes=[
             pltpu.VMEM((n_ch, CHUNKS, per, tokens, wide), jnp.bfloat16),
             pltpu.VMEM((n_ctx, rows, channels), jnp.bfloat16),
             pltpu.VMEM((chips, wide, channels), jnp.float32),
             pltpu.VMEM((2, chips, wide, channels), jnp.bfloat16),
             pltpu.VMEM((CHUNKS, chips, wide, channels), jnp.bfloat16),
-            pltpu.VMEM((CHUNKS, chips, wide, channels), jnp.bfloat16),
+            pltpu.VMEM((CHUNKS, chips - 1, wide, channels), jnp.bfloat16),
             dma((CHUNKS + 1, per)),
             dma((CHUNKS, hops, 2)),
             dma((CHUNKS, hops, 2)),
@@ -286,11 +315,81 @@
             dma((CHUNKS, chips)),
             dma((CHUNKS, chips)),
             dma((CHUNKS, chips)),
+            dma((2,)),
         ],
         compiler_params=pltpu.CompilerParams(
             collective_id=0, has_side_effects=True, vmem_limit_bytes=62 * 2**20
         ),
-    )(cotangent, proj_weight, gated)
+    )(cotangent, proj_weight, gated, query_act)
+
+
+def sum_kernel(n_ctx, x, out, arrived, r_send, r_recv, g_send, g_recv):
+    ctx = lax.axis_index("ctx")
+    ch = lax.axis_index("ch")
+    share = x.shape[0] // n_ctx
+    barrier = pltpu.get_barrier_semaphore()
+
+    def peer(off):
+        return (ctx + off) % n_ctx
+
+    def piece(i):
+        return pl.ds(pl.multiple_of(i * share, share), share)
+
+    @pl.loop(1, n_ctx)
+    def _(off):
+        pl.semaphore_signal(barrier, inc=1, device_id=(peer(off), ch), device_id_type=MESH)
+
+    pl.semaphore_wait(barrier, n_ctx - 1)
+
+    def scatter(off):
+        return pltpu.make_async_remote_copy(
+            x.at[piece(peer(off))], arrived.at[off - 1], r_send.at[off - 1], r_recv.at[off - 1],
+            device_id=(peer(off), ch), device_id_type=MESH)
+
+    def gather(off):
+        return pltpu.make_async_remote_copy(
+            out.at[piece(ctx)], out.at[piece(ctx)], g_send.at[off - 1], g_recv.at[off - 1],
+            device_id=(peer(off), ch), device_id_type=MESH)
+
+    def gathered(off):
+        source = piece(peer(n_ctx - off))
+        return pltpu.make_async_remote_copy(
+            out.at[source], out.at[source], g_send.at[off - 1], g_recv.at[off - 1],
+            device_id=(peer(off), ch), device_id_type=MESH)
+
+    @pl.loop(1, n_ctx)
+    def _(off):
+        scatter(off).start()
+
+    total = x[piece(ctx), :]
+    for off in range(1, n_ctx):
+        scatter(off).wait_recv()
+        total += arrived[off - 1]
+    out[piece(ctx), :] = total
+
+    @pl.loop(1, n_ctx)
+    def _(off):
+        gather(off).start()
+
+    @pl.loop(1, n_ctx)
+    def _(off):
+        gathered(off).wait_recv()
+        gather(off).wait_send()
+        scatter(off).wait_send()
+
+
+def summed_over_tokens(x):
+    n_ctx = lax.axis_size("ctx")
+    dma = pltpu.SemaphoreType.DMA
+    return pl.pallas_call(
+        functools.partial(sum_kernel, n_ctx),
+        out_shape=jax.ShapeDtypeStruct(x.shape, x.dtype),
+        in_specs=[pl.BlockSpec(memory_space=pltpu.VMEM)],
+        out_specs=pl.BlockSpec(memory_space=pltpu.VMEM),
+        scratch_shapes=[pltpu.VMEM((n_ctx - 1, x.shape[0] // n_ctx, x.shape[1]), x.dtype)]
+        + [dma((n_ctx - 1,))] * 4,
+        compiler_params=pltpu.CompilerParams(collective_id=1, has_side_effects=True),
+    )(x)
 
 
 def shards(query_act, key_act, value_act, filters, proj_weight, cotangent):
@@ -307,15 +406,13 @@
     prod_spec = forward(table[:, :TAPS], before) + forward(table[:, TAPS:], product)
     mixed = backward(inverse[TAPS:], times(prod_spec, filt_spec))
     gated = (query_f * mixed).astype(jnp.bfloat16)
-    grad_mix, grad_proj = exchange(cotangent, proj_weight, gated)
+    grad_mix, grad_gate, after, grad_proj = exchange(cotangent, proj_weight, gated, query_act)
     grad_query = (grad_mix * mixed).astype(jnp.bfloat16)
-    grad_gate = (grad_mix * query_f).astype(jnp.bfloat16)
-    after = from_behind(grad_gate[:TAPS], "ctx", -1)
     own_spec = forward(table[:, :tokens], grad_gate)
     gate_spec = own_spec + forward(table[:, tokens:], after)
     lags = inverse[TAPS - np.arange(TAPS)]
     local_filter = backward(lags, times_conj(prod_spec, own_spec))
-    grad_filter = lax.psum(local_filter, "ctx").T
+    grad_filter = summed_over_tokens(local_filter).T
     grad_prod = backward(inverse[:tokens], times_conj(gate_spec, filt_spec))
     grad_key = (grad_prod * value_f).astype(jnp.bfloat16)
     grad_value = (grad_prod * key_f).astype(jnp.bfloat16)

time: 319 us -> 277 us (0.87)
  waiting for transfers between devices: 45.6 us -> 0.01 us
  between operations: 14.4 us -> 1 us
  Pallas kernels: 213 us -> 226 us
  matrix products: 17.3 us -> 24.8 us
    psum x1 -> x0, waiting for transfers between devices: 45.6 us -> none  [shards(): grad_filter = lax.psum(local_filter, 'ctx').T]
    pallas_call x0 -> x1, Pallas kernels: none -> 23.3 us  [summed_over_tokens(): pl.pallas_call(functools.partial(sum_kernel, n_ctx), out_shape=jax.ShapeD...]
    pallas_call x1, Pallas kernels: 213 us -> 203 us  [exchange(): pl.pallas_call(functools.partial(exchange_kernel, n_ctx, n_ch), out_shape...]
    dot_general x19, matrix products: 17.3 us -> 24.8 us  [dot32(): return jnp.dot(a, b, preferred_element_type=jnp.float32)]
    unnamed x58 -> x64, local copies, waits for them, and re-layouts: 17.7 us -> 15.8 us
  transfers between devices with their start and end apart: 3 -> 1, of which waited for: 1 -> 0; matrix products, arithmetic and copies ran while one was open for 4% -> 1% of each run, Pallas kernels for 0% -> 0%
where the time goes in v3:
time: 277 us; the launch traced here: 276 us
  Pallas kernels  226 us (82%)
  matrix products  24.8 us (9%)
  local copies, waits for them, and re-layouts  15.9 us (6%)
  other arithmetic  5.55 us (2%)
    pallas_call x1, Pallas kernels, exchange(): pl.pallas_call(functools.partial(exchange_kernel, n_ctx, n_ch), out_shape...  203 us
    dot_general x19, matrix products, dot32(): return jnp.dot(a, b, preferred_element_type=jnp.float32)  24.8 us
    pallas_call x1, Pallas kernels, summed_over_tokens(): pl.pallas_call(functools.partial(sum_kernel, n_ctx), out_shape=jax.ShapeD...  23.3 us
    unnamed x64, local copies, waits for them, and re-layouts  15.8 us
  transfers between devices with their start and end apart: 1, of which 0 were waited for; matrix products, arithmetic and copies ran while one was open for 1% of the time, Pallas kernels for 0%

profile of v3, /device:TPU:0, one launch (start us, length us, event | category | flops | bytes accessed | tf_op | source)
XLA Modules:
  0.0 275.9 jit_solution(12249559865499618819)
XLA Ops:
  0.7 1.6 copy.19
  2.3 0.5 copy.20
  3.3 2.5 collective-permute-start
  5.8 0.9 fusion.34
  7.7 0.5 convolution_add_fusion
  8.2 0.6 copy-done.23
  8.7 0.9 fusion.33
  10.1 0.6 add_add_fusion.1
  10.8 0.8 multiply_subtract_fusion.2
  11.6 0.9 copy-done.4
  12.5 1.0 fusion.10
  13.6 1.0 fusion.13
  14.8 2.7 multiply_convert_fusion.1
  17.6 202.9 %shard_map.173 = (f32[512,1024]{1,0:T(8,128)}, bf16[512,1024]{1,0:T(8,128)(2,1)}, bf16[128,1024]{1,0:T(8,128)(2,1)}, f32[1024,1024]{1,0:T(8,128)}) custom-call(bf16[512,2048]{1,0:T(8,128)(2,1)} %cot.1, bf16[1024,1024]{1,0:T(8,128)(2,1)} %weight.1, bf16[512,1024]{1,0:T(8,128)(2,1)} %get-tuple-element.26.gated, bf16[512,1024]{1,0:T(8,128)(2,1)} %query.1), custom_call_target="tpu_custom_call" | custom-call | tf_op jit(solution)/shard_map/pallas_call | solution.py:285
  220.5 2.2 fusion.36
  222.8 0.8 convolution_add_fusion.1
  223.6 0.9 copy-done.5
  224.5 0.8 multiply_add_fusion
  226.3 0.5 add_add_fusion
  226.8 1.2 copy-done.3
  228.0 0.6 multiply_add_fusion.1
  229.1 2.4 fusion.6
  231.5 2.4 fusion.17
  234.7 0.5 copy-done.27
  235.2 1.2 convolution_add_fusion.2.x
  236.4 23.3 %shard_map.174 = f32[128,1024]{1,0:T(8,128)} custom-call(f32[128,1024]{1,0:T(8,128)} %convolution_add_fusion.2.x), custom_call_target="tpu_custom_call" | custom-call | tf_op jit(solution)/shard_map/pallas_call | solution.py:384
  259.7 2.0 copy.28
  261.7 5.4 %fusion.3 = (bf16[512,1024]{0,1:T(8,128)(2,1)}, bf16[512,1024]{0,1:T(8,128)(2,1)}) fusion(bf16[512,1024]{0,1:T(8,128)(2,1)} %copy-done.6, bf16[512,1024]{0,1:T(8,128)(2,1)} %copy-done.7, bf16[512,640]{1,0:T(8,128)(2,1)S(1)} %copy-done.18, f32[320,1024]{1,0:T(8,128)S(1)} %get-tuple-element.21, f32[320,1024]{1,0:T(8,128)S(1)} %get-tuple-element.20, ...), kind=kOutput, calls=%fused_computation.14 | convolution fusion | flops 677904384 | bytes 11665408 | tf_op jit(solution)/shard_map/dot_general | solution.py:34
  267.2 2.4 copy.27
  269.6 1.3 copy.26
  270.9 3.0 %multiply_convert_fusion = bf16[512,1024]{1,0:T(8,128)(2,1)} fusion(f32[512,1024]{1,0:T(8,128)} %get-tuple-element.9, f32[512,1024]{1,0:T(8,128)S(1)} %copy-done.8), kind=kLoop, calls=%fused_computation.19 | loop fusion | flops 1048576 | bytes 5242880 | tf_op jit(solution)/shard_map/convert_element_type | solution.py:410
  273.9 2.0 copy.35
  (61 shorter events, 4.5 us)
Async XLA Ops:
  0.6 6.1 %copy-start = (bf16[1024,128]{1,0:T(8,128)(2,1)S(1)}, bf16[1024,128]{1,0:T(8,128)(2,1)}, u32[]{:S(2)}) copy-start(bf16[1024,128]{1,0:T(8,128)(2,1)} %param.17) | copy-start | bytes 786436
  0.6 1.6 copy-start.17
  2.3 1.0 copy-start.6
  2.8 3.9 %copy-start.7 = (bf16[512,1024]{0,1:T(8,128)(2,1)}, bf16[512,1024]{0,1:T(8,128)(2,1)S(1)}, u32[]{:S(2)}) copy-start(bf16[512,1024]{0,1:T(8,128)(2,1)S(1)} %copy.20) | copy-start | bytes 3145732
  2.8 3.0 %copy-start.22 = (bf16[640,512]{1,0:T(8,128)(2,1)S(1)}, bf16[640,512]{1,0:T(8,128)(2,1)}, u32[]{:S(2)}) copy-start(bf16[640,512]{1,0:T(8,128)(2,1)} %constant.28) | copy-start | bytes 1966084
  3.3 3.4 %copy-start.25 = (bf16[640,128]{1,0:T(8,128)(2,1)S(1)}, bf16[640,128]{1,0:T(8,128)(2,1)}, u32[]{:S(2)}) copy-start(bf16[640,128]{1,0:T(8,128)(2,1)} %constant.21) | copy-start | bytes 491524
  3.3 6.3 %collective-permute-start = (bf16[128,1024]{0,1:T(8,128)(2,1)S(1)}, bf16[128,1024]{0,1:T(8,128)(2,1)S(1)}, u32[]{:S(2)}, u32[]{:S(2)}) collective-permute-start(bf16[128,1024]{0,1:T(8,128)(2,1)S(1)} %slice.40), channel_id=1, source_target_pairs={{0,4},{4,8},{8,12},{12,16},{16,20},{20,24},{24,28},{1,5},{5,9},{9,... | collective-permute-start | bytes 786440 | tf_op jit(solution)/shard_map/ppermute | solution.py:17
  6.7 0.9 copy-start.19
  7.7 1.1 copy-start.23
  8.7 2.0 copy-start.2
  10.8 1.8 copy-start.4
  10.8 1.7 copy-start.21
  12.5 1.1 copy-start.13
  13.6 1.2 copy-start.11
  17.6 202.9 %copy-start.15 = (bf16[640,512]{1,0:T(8,128)(2,1)S(1)}, bf16[640,512]{1,0:T(8,128)(2,1)}, u32[]{:S(2)}) copy-start(bf16[640,512]{1,0:T(8,128)(2,1)} %constant.33) | copy-start | bytes 1966084
  220.5 2.2 copy-start.12
  220.5 2.2 copy-start.20
  222.7 1.7 copy-start.5
  224.5 0.9 copy-start.16
  224.5 1.0 copy-start.26
  225.3 1.0 copy-start.28
  226.3 1.7 copy-start.3
  228.0 1.1 copy-start.14
  231.5 2.4 copy-start.24
  234.3 0.9 copy-start.27
  235.2 26.5 %copy-start.18 = (bf16[512,640]{1,0:T(8,128)(2,1)S(1)}, bf16[512,640]{1,0:T(8,128)(2,1)}, u32[]{:S(2)}) copy-start(bf16[512,640]{1,0:T(8,128)(2,1)} %constant.44) | copy-start | bytes 1966084
  267.2 2.4 copy-start.9
  267.2 3.7 %copy-start.8 = (f32[512,1024]{1,0:T(8,128)S(1)}, f32[512,1024]{1,0:T(8,128)}, u32[]{:S(2)}) copy-start(f32[512,1024]{1,0:T(8,128)} %get-tuple-element.27) | copy-start | bytes 6291460
  270.9 3.0 %copy-start.10 = (f32[1024,1024]{1,0:T(8,128)S(1)}, f32[1024,1024]{1,0:T(8,128)}, u32[]{:S(2)}) copy-start(f32[1024,1024]{1,0:T(8,128)} %get-tuple-element.37) | copy-start | bytes 12582916
  273.9 2.0 copy-start.1
